TPU v7x, 32 devices: a whole 2x2x4 slice. The times are simulated.
32 devices in a mesh: groups: 2 (over y), feat: 4 (over z), layer: 2 (over x), tok: 2 (over core).
Axes of the slice: x: 2, y: 2, z: 4, core: 2. Of those that a mesh axis runs over, the one named last changes fastest.
Arguments:
- residual_in: float32 [256, 2, 1792], P('groups', 'tok', 'feat'), parts along dimension 0, may hold values from -6 to 6
- attn_scale: float32 [2, 256], P('layer', 'groups'), parts along dimension 1, may hold values from 0.4 to 2.5
- mlp_scale: float32 [2, 256], P('layer', 'groups'), parts along dimension 1, may hold values from 0.4 to 2.5
- patterns: bfloat16 [2, 8, 4, 64, 64], P('layer', None, 'groups'), parts along dimension 2, may hold values from 0.0029907227 to 0.059814453
- lengths: int32 [4], P('groups'), parts along dimension 0, may hold values from 16 to 64
- value_proj: bfloat16 [2, 2, 1792, 1024], P('layer', 'tok', None, 'feat'), may hold values from -0.09375 to 0.09375
- out_proj: bfloat16 [2, 4, 256, 2, 2, 1792], P('layer', None, None, None, 'tok', 'feat'), may hold values from -0.125 to 0.125
- enc_weight: bfloat16 [2, 2, 1792, 512], P('layer', 'tok', None, 'feat'), may hold values from -0.09375 to 0.09375
- enc_bias: float32 [2, 512], P('layer', 'feat'), may hold values from -3 to 3
- dec_weight: bfloat16 [2, 2, 512, 2, 1792], P('layer', None, None, 'tok', 'feat'), may hold values from -0.25 to 0.25
- errors: float32 [2, 256, 2, 1792], P('layer', 'groups', 'tok', 'feat'), parts along dimension 1, may hold values from -4 to 4
- clamp_mode: int32 [2, 16384], P('layer', 'feat'), may hold values from 0 to 2
- clamp_index: int32 [2, 16384], P('layer', 'feat'), may hold values from 0 to 63
- clamp_values: float32 [64], replicated, may hold values from 0.25 to 3
- active_blocks: int32 [2, 4], P('layer', 'feat'), may hold values from 0 to 31
Outputs:
- residual_out: float32 [2, 256, 2, 1792], P('layer', 'groups', 'tok', 'feat'), parts along dimension 1
- features: bfloat16 [2, 256, 512], P('layer', 'groups', 'feat'), parts along dimension 1
There are 2 independent parts, one for each index of `groups`. A program takes and returns all parts, laid end to end along the dimension named above; an argument that names none is the same for every part. Nothing has to cross between parts.
Inputs may be any that keep to these rules, and one draw needn't show every extreme that they name: `clamp_mode`: 0 leaves a feature free, 1 sets it to its table value, 2 multiplies it by its table value. `lengths`: positions at or past a prompt's length are padding.
All inputs are finite; a program needn't handle non-finite values.
Results may differ from a plain program's by a relative error of at most 0.018.
Values may be sent and summed in bfloat16 or wider, within the bound.
A program may use at most 64 MiB of HBM per device.

v0:
```python
import jax
import jax.numpy as jnp
from jax import lax
from jax.sharding import PartitionSpec as P


def passed_along(value, axis, steps):
    count = lax.axis_size(axis)
    initial, last = (max(0, -steps), min(count, count - steps))
    return lax.ppermute(value, axis, [(source, source + steps) for source in range(initial, last)])


def columns(normed_rows):
    return lax.all_gather(normed_rows, "feat", axis=1, tiled=True)


def halves(partial_sum):
    return lax.psum(partial_sum, "tok")


def pick_block(lookup_table, chosen, block_len):
    shaped = lookup_table.reshape(-1, block_len)
    return lax.dynamic_slice_in_dim(shaped, chosen, 1, 0)[0]


def local(
    residual_in,
    attn_scale,
    mlp_scale,
    patterns,
    lengths,
    value_proj,
    out_proj,
    enc_weight,
    enc_bias,
    dec_weight,
    errors,
    clamp_mode,
    clamp_index,
    clamp_values,
    active_blocks,
):
    layer_count = lax.axis_size("layer")
    my_layer = lax.axis_index("layer")
    my_range = lax.axis_index("feat")
    seq_len = patterns.shape[3]
    prompt_count = patterns.shape[2]
    head_dim = out_proj.shape[2]
    per_group = out_proj.shape[3]
    kv_cols = value_proj.shape[3]
    width_cols = residual_in.shape[2]
    block_len = enc_bias.shape[1]
    total_rows = residual_in.shape[0]
    split_count = 1
    block_rows = seq_len // split_count
    micro_count = prompt_count * split_count
    section_count = layer_count + micro_count - 1
    source_rows = residual_in[:, 0, :]
    error_rows = errors[0, :, 0, :]
    value_weight = value_proj[0, 0]
    out_weight = out_proj[0].reshape(-1, width_cols)
    enc_rows = enc_weight[0, 0]
    enc_shift = enc_bias[0]
    dec_rows = dec_weight[0, :, :, 0, :]
    chosen = active_blocks[0, 0]
    modes = pick_block(clamp_mode[0], chosen, block_len)
    table_pick = pick_block(clamp_index[0], chosen, block_len)
    table_ids = jnp.arange(clamp_values.shape[0], dtype=jnp.int32)
    levels = jnp.sum(
        jnp.where(table_pick[:, None] == table_ids[None, :], clamp_values[None, :], 0.0), axis=1
    )
    group_id = my_range * kv_cols // head_dim
    group_pat = lax.dynamic_slice_in_dim(patterns[0], group_id * per_group, per_group, 0)
    positions = jnp.arange(seq_len, dtype=jnp.int32)
    scale_attn = attn_scale[0]
    scale_mlp = mlp_scale[0]

    def add_heads(piece):
        return jnp.dot(piece, out_weight, preferred_element_type=jnp.float32)

    def add_writes(piece):
        return jnp.einsum("rf,tfc->trc", piece, dec_rows, preferred_element_type=jnp.float32)

    def section(step_num, carry):
        recv_rows, links, value_cache, kept_rows, kept_feats = carry
        micro_raw = step_num - my_layer
        is_live = (micro_raw >= 0) & (micro_raw < micro_count)
        micro_num = jnp.clip(micro_raw, 0, micro_count - 1)
        prompt_num = micro_num // split_count
        block_num = micro_num % split_count
        first_row = micro_num * block_rows
        first_pos = block_num * block_rows
        start_rows = lax.dynamic_slice_in_dim(source_rows, first_row, block_rows, 0)
        rows_in = jnp.where(my_layer == 0, start_rows, recv_rows)
        row_attn = lax.dynamic_slice_in_dim(scale_attn, first_row, block_rows, 0)
        normed = (rows_in * row_attn[:, None]).astype(jnp.bfloat16)
        values = halves(
            jnp.dot(columns(normed), value_weight, preferred_element_type=jnp.float32)
        ).astype(jnp.bfloat16)
        value_cache = values
        query_pos = first_pos + jnp.arange(block_rows, dtype=jnp.int32)
        prompt_len = lax.dynamic_index_in_dim(lengths, prompt_num, 0, keepdims=False)
        keep_keys = (positions[None, :] <= query_pos[:, None]) & (positions[None, :] < prompt_len)
        block_pat = lax.dynamic_slice(
            group_pat, (0, prompt_num, first_pos, 0), (per_group, 1, block_rows, seq_len)
        )[:, 0]
        block_pat = jnp.where(keep_keys[None], block_pat, jnp.zeros_like(block_pat))
        head_out = (
            jnp.einsum("uqk,kc->qcu", block_pat, value_cache, preferred_element_type=jnp.float32)
            .astype(jnp.bfloat16)
            .reshape(block_rows, -1)
        )
        attention = add_heads(lax.all_gather(head_out, "feat", axis=1, tiled=True))
        middle = rows_in + attention
        row_mlp = lax.dynamic_slice_in_dim(scale_mlp, first_row, block_rows, 0)
        normed_mlp = (middle * row_mlp[:, None]).astype(jnp.bfloat16)
        preact = (
            halves(jnp.dot(columns(normed_mlp), enc_rows, preferred_element_type=jnp.float32))
            + enc_shift
        )
        active = jnp.maximum(preact, 0.0)
        clamped = jnp.where(modes == 1, levels, jnp.where(modes == 2, active * levels, active))
        live_rows = query_pos < prompt_len
        block_feats = jnp.where(live_rows[:, None], clamped, 0.0).astype(jnp.bfloat16)
        writes = add_writes(lax.all_gather(block_feats, "feat", axis=1, tiled=True))
        error_block = lax.dynamic_slice_in_dim(error_rows, first_row, block_rows, 0)
        acc_in = jnp.where(my_layer == 0, jnp.zeros_like(links), links)
        running = acc_in + writes
        recon = lax.dynamic_index_in_dim(running, my_layer, 0, keepdims=False)
        rows_next = middle + recon + error_block
        recv_rows, links = passed_along((rows_next, running), "layer", 1)
        old_rows = lax.dynamic_slice_in_dim(kept_rows, first_row, block_rows, 0)
        kept_rows = lax.dynamic_update_slice_in_dim(
            kept_rows, jnp.where(is_live, rows_next, old_rows), first_row, 0
        )
        old_feats = lax.dynamic_slice_in_dim(kept_feats, first_row, block_rows, 0)
        kept_feats = lax.dynamic_update_slice_in_dim(
            kept_feats, jnp.where(is_live, block_feats, old_feats), first_row, 0
        )
        return (recv_rows, links, value_cache, kept_rows, kept_feats)

    link_start = jnp.zeros((layer_count, block_rows, width_cols), jnp.float32)
    initial = (
        jnp.zeros((block_rows, width_cols), jnp.float32),
        link_start,
        jnp.zeros((seq_len, kv_cols), jnp.bfloat16),
        jnp.zeros((total_rows, width_cols), jnp.float32),
        jnp.zeros((total_rows, block_len), jnp.bfloat16),
    )
    final = lax.fori_loop(0, section_count, section, initial)
    return (final[3][None, :, None, :], final[4][None])


def solution(mesh):
    return jax.shard_map(
        local,
        mesh=mesh,
        in_specs=(
            P("groups", "tok", "feat"),
            P("layer", "groups"),
            P("layer", "groups"),
            P("layer", None, "groups", None, None),
            P("groups"),
            P("layer", "tok", None, "feat"),
            P("layer", None, None, None, "tok", "feat"),
            P("layer", "tok", None, "feat"),
            P("layer", "feat"),
            P("layer", None, None, "tok", "feat"),
            P("layer", "groups", "tok", "feat"),
            P("layer", "feat"),
            P("layer", "feat"),
            P(),
            P("layer", "feat"),
        ),
        out_specs=(P("layer", "groups", "tok", "feat"), P("layer", "groups", "feat")),
        check_vma=False,
    )
```

profile of v0, /device:TPU:0, one launch (start us, length us, event | category | flops | bytes accessed | tf_op | source)
XLA Modules:
  0.0 265.3 jit_solution(8046609144955655287)
XLA Ops:
  0.7 0.9 copy-done
  2.2 0.7 fusion.19
  3.0 0.7 select_reduce_fusion
  3.7 6.1 %copy.43 = bf16[1,4,256,2,1,448]{5,3,2,1,4,0:T(2,128)(2,1)} copy(bf16[1,4,256,2,1,448]{2,5,4,3,1,0:T(8,128)(2,1)} %param.23) | data formatting | bytes 3670016 | tf_op args[6]
  9.9 3.5 %reshape_squeeze.9 = bf16[2048,448]{1,0:T(8,128)(2,1)S(1)} reshape(bf16[1,4,256,2,1,448]{5,3,2,1,4,0:T(2,128)(2,1)} %copy.43) | data formatting | bytes 3670016 | tf_op jit(solution)/shard_map/reshape;squeeze | solution.py:61
  13.5 0.8 copy.44
  14.4 0.7 broadcast.116
  15.1 0.7 broadcast_in_dim.131
  15.9 247.6 %while.23 = (s32[]{:T(128)}, f32[64,448]{1,0:T(8,128)S(1)}, f32[2,64,448]{2,1,0:T(8,128)}, f32[128,448]{1,0:T(8,128)}, bf16[128,128]{1,0:T(8,128)(2,1)S(1)}, /*i...) while((s32[]{:T(128)}, f32[64,448]{1,0:T(8,128)S(1)}, ...), condition=%wide.region_4.5_spmd.clone.clone, body=%wide.region_1.4_spmd.clone.clone.sunk | while | flops 268976448 | bytes 11732813 | solution.py:150
  16.1 15.7 %all-gather.6 = bf16[4,448,64]{1,2,0:T(8,128)(2,1)S(1)} all-gather(bf16[1,448,64]{1,2,0:T(8,128)(2,1)S(1)} %fusion.57), channel_id=1, replica_groups=mesh['groups'=2,'feat'=4,'layer'=2,'tok'=2] {'feat'}, dimensions={0}, use_global_device_ids=true | all-gather | bytes 286720 | tf_op jit(solution)/shard_map/while/body/eval_jaxpr/all_gather | solution.py:14
  31.9 0.3 reshape.85
  32.2 1.5 fusion.58
  33.7 3.6 %psum.34 = bf16[64,256]{1,0:T(8,128)(2,1)S(1)} all-reduce(f32[64,256]{1,0:T(8,128)S(1)} %fusion.58), channel_id=1, replica_groups=mesh['groups'=2,'feat'=4,'layer'=2,'tok'=2] {'tok'}, use_global_device_ids=true, to_apply=%region_2.2 | all-reduce | flops 16384 | bytes 98304 | tf_op jit(solution)/shard_map/while/body/eval_jaxpr/psum | solution.py:18
  37.3 0.7 dynamic_slice.163
  37.9 0.7 iota_compare_fusion.4
  38.9 16.6 %all_gather.48 = bf16[64,2048]{0,1:T(8,128)(2,1)S(1)} all-gather(bf16[64,512]{0,1:T(8,128)(2,1)S(1)} %bitcast.101), channel_id=1, replica_groups=mesh['groups'=2,'feat'=4,'layer'=2,'tok'=2] {'feat'}, dimensions={1}, use_global_device_ids=true | all-gather | bytes 327680 | tf_op jit(solution)/shard_map/while/body/eval_jaxpr/all_gather | solution.py:113
  55.6 0.5 convolution_add_fusion.2
  56.2 14.5 %all-gather.7 = bf16[4,448,64]{1,2,0:T(8,128)(2,1)S(1)} all-gather(bf16[1,448,64]{1,2,0:T(8,128)(2,1)S(1)} %fusion.61), channel_id=1, replica_groups=mesh['groups'=2,'feat'=4,'layer'=2,'tok'=2] {'feat'}, dimensions={0}, use_global_device_ids=true | all-gather | bytes 286720 | tf_op jit(solution)/shard_map/while/body/eval_jaxpr/all_gather | solution.py:14
  70.9 0.3 reshape.86
  71.2 1.2 fusion.62
  72.4 3.4 %psum.35 = f32[64,128]{1,0:T(8,128)S(1)} all-reduce(f32[64,128]{1,0:T(8,128)S(1)} %fusion.62), channel_id=1, replica_groups=mesh['groups'=2,'feat'=4,'layer'=2,'tok'=2] {'tok'}, use_global_device_ids=true, to_apply=%region_3.3 | all-reduce | flops 8192 | bytes 65536 | tf_op jit(solution)/shard_map/while/body/eval_jaxpr/psum | solution.py:18
  76.0 12.0 %all_gather.49 = bf16[64,512]{1,0:T(8,128)(2,1)S(1)} all-gather(bf16[64,128]{1,0:T(8,128)(2,1)S(1)} %get-tuple-element.762), channel_id=1, replica_groups=mesh['groups'=2,'feat'=4,'layer'=2,'tok'=2] {'feat'}, dimensions={1}, use_global_device_ids=true | all-gather | bytes 81920 | tf_op jit(solution)/shard_map/while/body/eval_jaxpr/all_gather | solution.py:125
  88.0 1.6 fusion.63
  89.5 4.1 %collective-permute-start.1 = (f32[2,64,448]{2,1,0:T(8,128)S(1)}, f32[2,64,448]{2,1,0:T(8,128)}, u32[]{:S(2)}, u32[]{:S(2)}) collective-permute-start(f32[2,64,448]{2,1,0:T(8,128)S(1)} %fusion.63), channel_id=1, source_target_pairs={{0,2},{1,3},{4,6},{5,7},{8,10},{9,11},{12,14},{13,15},{16,18},{17,... | collective-permute-start | bytes 688136 | tf_op jit(solution)/shard_map/while/body/eval_jaxpr/ppermute | solution.py:10
  93.7 1.6 select_dynamic-update-slice_fusion.5
  95.3 1.3 collective-permute-start
  96.6 3.0 %collective-permute-done = f32[64,448]{1,0:T(8,128)S(1)} collective-permute-done((f32[64,448]{1,0:T(8,128)S(1)}, f32[64,448]{1,0:T(8,128)S(1)}, u32[]{:S(2)}, u32[]{:S(2)}) %collective-permute-start) | collective-permute-done | bytes 114720 | tf_op jit(solution)/shard_map/while/body/eval_jaxpr/ppermute | solution.py:10
  99.8 14.3 %all-gather.6 = bf16[4,448,64]{1,2,0:T(8,128)(2,1)S(1)} all-gather(bf16[1,448,64]{1,2,0:T(8,128)(2,1)S(1)} %fusion.57), channel_id=1, replica_groups=mesh['groups'=2,'feat'=4,'layer'=2,'tok'=2] {'feat'}, dimensions={0}, use_global_device_ids=true | all-gather | bytes 286720 | tf_op jit(solution)/shard_map/while/body/eval_jaxpr/all_gather | solution.py:14
  114.3 0.3 reshape.85
  114.6 1.5 fusion.58
  116.1 3.6 %psum.34 = bf16[64,256]{1,0:T(8,128)(2,1)S(1)} all-reduce(f32[64,256]{1,0:T(8,128)S(1)} %fusion.58), channel_id=1, replica_groups=mesh['groups'=2,'feat'=4,'layer'=2,'tok'=2] {'tok'}, use_global_device_ids=true, to_apply=%region_2.2 | all-reduce | flops 16384 | bytes 98304 | tf_op jit(solution)/shard_map/while/body/eval_jaxpr/psum | solution.py:18
  119.7 0.7 dynamic_slice.163
  120.3 0.7 iota_compare_fusion.4
  121.3 16.2 %all_gather.48 = bf16[64,2048]{0,1:T(8,128)(2,1)S(1)} all-gather(bf16[64,512]{0,1:T(8,128)(2,1)S(1)} %bitcast.101), channel_id=1, replica_groups=mesh['groups'=2,'feat'=4,'layer'=2,'tok'=2] {'feat'}, dimensions={1}, use_global_device_ids=true | all-gather | bytes 327680 | tf_op jit(solution)/shard_map/while/body/eval_jaxpr/all_gather | solution.py:113
  137.6 0.5 convolution_add_fusion.2
  138.2 13.8 %all-gather.7 = bf16[4,448,64]{1,2,0:T(8,128)(2,1)S(1)} all-gather(bf16[1,448,64]{1,2,0:T(8,128)(2,1)S(1)} %fusion.61), channel_id=1, replica_groups=mesh['groups'=2,'feat'=4,'layer'=2,'tok'=2] {'feat'}, dimensions={0}, use_global_device_ids=true | all-gather | bytes 286720 | tf_op jit(solution)/shard_map/while/body/eval_jaxpr/all_gather | solution.py:14
  152.2 0.3 reshape.86
  152.5 1.2 fusion.62
  153.7 3.4 %psum.35 = f32[64,128]{1,0:T(8,128)S(1)} all-reduce(f32[64,128]{1,0:T(8,128)S(1)} %fusion.62), channel_id=1, replica_groups=mesh['groups'=2,'feat'=4,'layer'=2,'tok'=2] {'tok'}, use_global_device_ids=true, to_apply=%region_3.3 | all-reduce | flops 8192 | bytes 65536 | tf_op jit(solution)/shard_map/while/body/eval_jaxpr/psum | solution.py:18
  157.3 12.0 %all_gather.49 = bf16[64,512]{1,0:T(8,128)(2,1)S(1)} all-gather(bf16[64,128]{1,0:T(8,128)(2,1)S(1)} %get-tuple-element.762), channel_id=1, replica_groups=mesh['groups'=2,'feat'=4,'layer'=2,'tok'=2] {'feat'}, dimensions={1}, use_global_device_ids=true | all-gather | bytes 81920 | tf_op jit(solution)/shard_map/while/body/eval_jaxpr/all_gather | solution.py:125
  169.3 1.6 fusion.63
  170.8 5.0 %collective-permute-start.1 = (f32[2,64,448]{2,1,0:T(8,128)S(1)}, f32[2,64,448]{2,1,0:T(8,128)}, u32[]{:S(2)}, u32[]{:S(2)}) collective-permute-start(f32[2,64,448]{2,1,0:T(8,128)S(1)} %fusion.63), channel_id=1, source_target_pairs={{0,2},{1,3},{4,6},{5,7},{8,10},{9,11},{12,14},{13,15},{16,18},{17,... | collective-permute-start | bytes 688136 | tf_op jit(solution)/shard_map/while/body/eval_jaxpr/ppermute | solution.py:10
  175.9 1.7 select_dynamic-update-slice_fusion.5
  177.5 1.3 collective-permute-start
  178.8 3.0 %collective-permute-done = f32[64,448]{1,0:T(8,128)S(1)} collective-permute-done((f32[64,448]{1,0:T(8,128)S(1)}, f32[64,448]{1,0:T(8,128)S(1)}, u32[]{:S(2)}, u32[]{:S(2)}) %collective-permute-start) | collective-permute-done | bytes 114720 | tf_op jit(solution)/shard_map/while/body/eval_jaxpr/ppermute | solution.py:10
  182.0 13.8 %all-gather.6 = bf16[4,448,64]{1,2,0:T(8,128)(2,1)S(1)} all-gather(bf16[1,448,64]{1,2,0:T(8,128)(2,1)S(1)} %fusion.57), channel_id=1, replica_groups=mesh['groups'=2,'feat'=4,'layer'=2,'tok'=2] {'feat'}, dimensions={0}, use_global_device_ids=true | all-gather | bytes 286720 | tf_op jit(solution)/shard_map/while/body/eval_jaxpr/all_gather | solution.py:14
  196.0 0.3 reshape.85
  196.3 1.5 fusion.58
  197.7 3.6 %psum.34 = bf16[64,256]{1,0:T(8,128)(2,1)S(1)} all-reduce(f32[64,256]{1,0:T(8,128)S(1)} %fusion.58), channel_id=1, replica_groups=mesh['groups'=2,'feat'=4,'layer'=2,'tok'=2] {'tok'}, use_global_device_ids=true, to_apply=%region_2.2 | all-reduce | flops 16384 | bytes 98304 | tf_op jit(solution)/shard_map/while/body/eval_jaxpr/psum | solution.py:18
  201.4 0.7 dynamic_slice.163
  202.0 0.7 iota_compare_fusion.4
  203.0 16.1 %all_gather.48 = bf16[64,2048]{0,1:T(8,128)(2,1)S(1)} all-gather(bf16[64,512]{0,1:T(8,128)(2,1)S(1)} %bitcast.101), channel_id=1, replica_groups=mesh['groups'=2,'feat'=4,'layer'=2,'tok'=2] {'feat'}, dimensions={1}, use_global_device_ids=true | all-gather | bytes 327680 | tf_op jit(solution)/shard_map/while/body/eval_jaxpr/all_gather | solution.py:113
  219.1 0.5 convolution_add_fusion.2
  219.7 13.8 %all-gather.7 = bf16[4,448,64]{1,2,0:T(8,128)(2,1)S(1)} all-gather(bf16[1,448,64]{1,2,0:T(8,128)(2,1)S(1)} %fusion.61), channel_id=1, replica_groups=mesh['groups'=2,'feat'=4,'layer'=2,'tok'=2] {'feat'}, dimensions={0}, use_global_device_ids=true | all-gather | bytes 286720 | tf_op jit(solution)/shard_map/while/body/eval_jaxpr/all_gather | solution.py:14
  233.8 0.3 reshape.86
  234.0 1.2 fusion.62
  235.3 3.4 %psum.35 = f32[64,128]{1,0:T(8,128)S(1)} all-reduce(f32[64,128]{1,0:T(8,128)S(1)} %fusion.62), channel_id=1, replica_groups=mesh['groups'=2,'feat'=4,'layer'=2,'tok'=2] {'tok'}, use_global_device_ids=true, to_apply=%region_3.3 | all-reduce | flops 8192 | bytes 65536 | tf_op jit(solution)/shard_map/while/body/eval_jaxpr/psum | solution.py:18
  238.8 12.0 %all_gather.49 = bf16[64,512]{1,0:T(8,128)(2,1)S(1)} all-gather(bf16[64,128]{1,0:T(8,128)(2,1)S(1)} %get-tuple-element.762), channel_id=1, replica_groups=mesh['groups'=2,'feat'=4,'layer'=2,'tok'=2] {'feat'}, dimensions={1}, use_global_device_ids=true | all-gather | bytes 81920 | tf_op jit(solution)/shard_map/while/body/eval_jaxpr/all_gather | solution.py:125
  250.8 1.6 fusion.63
  252.4 5.1 %collective-permute-start.1 = (f32[2,64,448]{2,1,0:T(8,128)S(1)}, f32[2,64,448]{2,1,0:T(8,128)}, u32[]{:S(2)}, u32[]{:S(2)}) collective-permute-start(f32[2,64,448]{2,1,0:T(8,128)S(1)} %fusion.63), channel_id=1, source_target_pairs={{0,2},{1,3},{4,6},{5,7},{8,10},{9,11},{12,14},{13,15},{16,18},{17,... | collective-permute-start | bytes 688136 | tf_op jit(solution)/shard_map/while/body/eval_jaxpr/ppermute | solution.py:10
  257.5 1.7 select_dynamic-update-slice_fusion.5
  259.1 1.3 collective-permute-start
  260.4 3.0 %collective-permute-done = f32[64,448]{1,0:T(8,128)S(1)} collective-permute-done((f32[64,448]{1,0:T(8,128)S(1)}, f32[64,448]{1,0:T(8,128)S(1)}, u32[]{:S(2)}, u32[]{:S(2)}) %collective-permute-start) | collective-permute-done | bytes 114720 | tf_op jit(solution)/shard_map/while/body/eval_jaxpr/ppermute | solution.py:10
  263.5 1.8 copy.45
  (55 shorter events, 3.5 us)
Async XLA Ops:
  0.6 1.0 copy-start
  9.8 3.5 %copy-start.2 = (f32[128,1,448]{0,2,1:T(8,128)S(1)}, f32[128,1,448]{0,2,1:T(8,128)}, u32[]{:S(2)}) copy-start(f32[128,1,448]{0,2,1:T(8,128)} %param.17) | copy-start | bytes 688132
  9.8 3.7 %copy-start.3 = (f32[1,128,1,448]{1,3,2,0:T(8,128)S(1)}, f32[1,128,1,448]{1,3,2,0:T(8,128)}, u32[]{:S(2)}) copy-start(f32[1,128,1,448]{1,3,2,0:T(8,128)} %param.27) | copy-start | bytes 688132
  9.8 6.0 %copy-start.4 = (f32[1,128]{1,0:T(1,128)S(1)}, f32[1,128]{1,0:T(1,128)}, u32[]{:S(2)}) copy-start(f32[1,128]{1,0:T(1,128)} %param.25) | copy-start | bytes 1540
  9.8 6.0 %copy-start.5 = (f32[1,128]{1,0:T(1,128)S(1)}, f32[1,128]{1,0:T(1,128)}, u32[]{:S(2)}) copy-start(f32[1,128]{1,0:T(1,128)} %param.18) | copy-start | bytes 1540
  9.9 6.0 %copy-start.6 = (s32[2]{0:T(128)S(1)}, s32[2]{0:T(128)}, u32[]{:S(2)}) copy-start(s32[2]{0:T(128)} %param.21) | copy-start | bytes 28
  9.9 6.0 %copy-start.7 = (f32[1,128]{1,0:T(1,128)S(1)}, f32[1,128]{1,0:T(1,128)}, u32[]{:S(2)}) copy-start(f32[1,128]{1,0:T(1,128)} %param.19) | copy-start | bytes 1540
  89.5 10.1 %collective-permute-start.1 = (f32[2,64,448]{2,1,0:T(8,128)S(1)}, f32[2,64,448]{2,1,0:T(8,128)}, u32[]{:S(2)}, u32[]{:S(2)}) collective-permute-start(f32[2,64,448]{2,1,0:T(8,128)S(1)} %fusion.63), channel_id=1, source_target_pairs={{0,2},{1,3},{4,6},{5,7},{8,10},{9,11},{12,14},{13,15},{16,18},{17,... | collective-permute-start | bytes 688136 | tf_op jit(solution)/shard_map/while/body/eval_jaxpr/ppermute | solution.py:10
  95.3 4.3 %collective-permute-start = (f32[64,448]{1,0:T(8,128)S(1)}, f32[64,448]{1,0:T(8,128)S(1)}, u32[]{:S(2)}, u32[]{:S(2)}) collective-permute-start(f32[64,448]{1,0:T(8,128)S(1)} %get-tuple-element.763), channel_id=1, source_target_pairs={{0,2},{1,3},{4,6},{5,7},{8,10},{9,11},{12,14},{13,15},{16,18},{17,... | collective-permute-start | bytes 344072 | tf_op jit(solution)/shard_map/while/body/eval_jaxpr/ppermute | solution.py:10
  170.8 11.0 %collective-permute-start.1 = (f32[2,64,448]{2,1,0:T(8,128)S(1)}, f32[2,64,448]{2,1,0:T(8,128)}, u32[]{:S(2)}, u32[]{:S(2)}) collective-permute-start(f32[2,64,448]{2,1,0:T(8,128)S(1)} %fusion.63), channel_id=1, source_target_pairs={{0,2},{1,3},{4,6},{5,7},{8,10},{9,11},{12,14},{13,15},{16,18},{17,... | collective-permute-start | bytes 688136 | tf_op jit(solution)/shard_map/while/body/eval_jaxpr/ppermute | solution.py:10
  177.5 4.3 %collective-permute-start = (f32[64,448]{1,0:T(8,128)S(1)}, f32[64,448]{1,0:T(8,128)S(1)}, u32[]{:S(2)}, u32[]{:S(2)}) collective-permute-start(f32[64,448]{1,0:T(8,128)S(1)} %get-tuple-element.763), channel_id=1, source_target_pairs={{0,2},{1,3},{4,6},{5,7},{8,10},{9,11},{12,14},{13,15},{16,18},{17,... | collective-permute-start | bytes 344072 | tf_op jit(solution)/shard_map/while/body/eval_jaxpr/ppermute | solution.py:10
  252.4 11.1 %collective-permute-start.1 = (f32[2,64,448]{2,1,0:T(8,128)S(1)}, f32[2,64,448]{2,1,0:T(8,128)}, u32[]{:S(2)}, u32[]{:S(2)}) collective-permute-start(f32[2,64,448]{2,1,0:T(8,128)S(1)} %fusion.63), channel_id=1, source_target_pairs={{0,2},{1,3},{4,6},{5,7},{8,10},{9,11},{12,14},{13,15},{16,18},{17,... | collective-permute-start | bytes 688136 | tf_op jit(solution)/shard_map/while/body/eval_jaxpr/ppermute | solution.py:10
  259.1 4.3 %collective-permute-start = (f32[64,448]{1,0:T(8,128)S(1)}, f32[64,448]{1,0:T(8,128)S(1)}, u32[]{:S(2)}, u32[]{:S(2)}) collective-permute-start(f32[64,448]{1,0:T(8,128)S(1)} %get-tuple-element.763), channel_id=1, source_target_pairs={{0,2},{1,3},{4,6},{5,7},{8,10},{9,11},{12,14},{13,15},{16,18},{17,... | collective-permute-start | bytes 344072 | tf_op jit(solution)/shard_map/while/body/eval_jaxpr/ppermute | solution.py:10
  263.5 1.8 copy-start.1
where the time goes:
time: 266 us; the launch traced here: 265 us
  blocking collectives  192 us (72%)
  local copies, waits for them, and re-layouts  21.1 us (8%)
  starting transfers between devices  18.2 us (7%)
  matrix products  14.7 us (6%)
  waiting for transfers between devices  9.11 us (3%)
  other arithmetic  8.55 us (3%)
    all_gather x6, blocking collectives, columns(): return lax.all_gather(normed_rows, 'feat', axis=1, tiled=True)  85.9 us
    all_gather x3, blocking collectives, section(): attention = add_heads(lax.all_gather(head_out, 'feat', axis=1, tiled=True))  48.9 us
    all_gather x3, blocking collectives, section(): writes = add_writes(lax.all_gather(block_feats, 'feat', axis=1, tiled=True))  36 us
    psum x6, blocking collectives, halves(): return lax.psum(partial_sum, 'tok')  21.1 us
    ppermute x6, starting transfers between devices, passed_along(): lax.ppermute(value, axis, [(source, source + steps) for source in range(i...  18.2 us
    ppermute x6, waiting for transfers between devices, passed_along(): lax.ppermute(value, axis, [(source, source + steps) for source in range(i...  9.11 us
    unnamed x19, local copies, waits for them, and re-layouts  8.06 us
  transfers between devices with their start and end apart: 6, of which 3 were waited for; matrix products, arithmetic and copies ran while one was open for 2% of the time, Pallas kernels for 0%

commit v1 on v0

--- a/solution.py
+++ b/solution.py
@@ -2,6 +2,10 @@
 import jax.numpy as jnp
 from jax import lax
 from jax.sharding import PartitionSpec as P
+
+mark_the_entries = lambda block_here: jnp.concatenate(
+    lax.all_gather(block_here, axis_name="feat"), 1
+)
 
 
 def passed_along(value, axis, steps):
@@ -122,7 +126,7 @@
         clamped = jnp.where(modes == 1, levels, jnp.where(modes == 2, active * levels, active))
         live_rows = query_pos < prompt_len
         block_feats = jnp.where(live_rows[:, None], clamped, 0.0).astype(jnp.bfloat16)
-        writes = add_writes(lax.all_gather(block_feats, "feat", axis=1, tiled=True))
+        writes = add_writes(mark_the_entries(block_feats))
         error_block = lax.dynamic_slice_in_dim(error_rows, first_row, block_rows, 0)
         acc_in = jnp.where(my_layer == 0, jnp.zeros_like(links), links)
         running = acc_in + writes

time: 266 us -> 271 us (1.019)
  blocking collectives: 192 us -> 196 us
    all_gather x3, blocking collectives: 36 us -> 39.4 us  [lax.all_gather(block_here, axis_name='feat')]
where the time goes in v1:
time: 271 us; the launch traced here: 270 us
  blocking collectives  196 us (72%)
  local copies, waits for them, and re-layouts  21.3 us (8%)
  starting transfers between devices  18.3 us (7%)
  matrix products  14.7 us (5%)
  waiting for transfers between devices  9.11 us (3%)
  other arithmetic  8.55 us (3%)
    all_gather x6, blocking collectives, columns(): return lax.all_gather(normed_rows, 'feat', axis=1, tiled=True)  88 us
    all_gather x3, blocking collectives, section(): attention = add_heads(lax.all_gather(head_out, 'feat', axis=1, tiled=True))  47.8 us
    all_gather x3, blocking collectives, lax.all_gather(block_here, axis_name='feat')  39.4 us
    psum x6, blocking collectives, halves(): return lax.psum(partial_sum, 'tok')  21.1 us
    ppermute x6, starting transfers between devices, passed_along(): lax.ppermute(value, axis, [(source, source + steps) for source in range(i...  18.3 us
    ppermute x6, waiting for transfers between devices, passed_along(): lax.ppermute(value, axis, [(source, source + steps) for source in range(i...  9.11 us
    unnamed x19, local copies, waits for them, and re-layouts  8.06 us
  transfers between devices with their start and end apart: 6, of which 3 were waited for; matrix products, arithmetic and copies ran while one was open for 2% of the time, Pallas kernels for 0%

profile of v1, /device:TPU:0, one launch (start us, length us, event | category | flops | bytes accessed | tf_op | source)
XLA Modules:
  0.0 270.0 jit_solution(17759779088368684759)
XLA Ops:
  0.7 0.9 copy-done
  2.2 0.7 fusion.18
  3.0 0.7 select_reduce_fusion
  3.7 6.1 %copy.47 = bf16[1,4,256,2,1,448]{5,3,2,1,4,0:T(2,128)(2,1)} copy(bf16[1,4,256,2,1,448]{2,5,4,3,1,0:T(8,128)(2,1)} %param.23) | data formatting | bytes 3670016 | tf_op args[6]
  9.9 3.5 %reshape_squeeze.9 = bf16[2048,448]{1,0:T(8,128)(2,1)S(1)} reshape(bf16[1,4,256,2,1,448]{5,3,2,1,4,0:T(2,128)(2,1)} %copy.47) | data formatting | bytes 3670016 | tf_op jit(solution)/shard_map/reshape;squeeze | solution.py:65
  13.5 0.8 copy.48
  14.4 0.7 broadcast.116
  15.1 0.7 broadcast_in_dim.131
  15.9 252.4 %while.23 = (s32[]{:T(128)}, f32[64,448]{1,0:T(8,128)S(1)}, f32[2,64,448]{2,1,0:T(8,128)}, f32[128,448]{1,0:T(8,128)}, bf16[128,128]{1,0:T(8,128)(2,1)S(1)}, /*i...) while((s32[]{:T(128)}, f32[64,448]{1,0:T(8,128)S(1)}, ...), condition=%wide.region_4.5_spmd.clone.clone, body=%wide.region_1.4_spmd.clone.clone.sunk | while | flops 268976448 | bytes 11994957 | solution.py:154
  16.1 15.7 %all-gather.9 = bf16[4,448,64]{1,2,0:T(8,128)(2,1)S(1)} all-gather(bf16[1,448,64]{1,2,0:T(8,128)(2,1)S(1)} %fusion.57), channel_id=1, replica_groups=mesh['groups'=2,'feat'=4,'layer'=2,'tok'=2] {'feat'}, dimensions={0}, use_global_device_ids=true | all-gather | bytes 286720 | tf_op jit(solution)/shard_map/while/body/eval_jaxpr/all_gather | solution.py:18
  31.9 0.3 reshape.113
  32.2 1.5 fusion.58
  33.7 3.6 %psum.34 = bf16[64,256]{1,0:T(8,128)(2,1)S(1)} all-reduce(f32[64,256]{1,0:T(8,128)S(1)} %fusion.58), channel_id=1, replica_groups=mesh['groups'=2,'feat'=4,'layer'=2,'tok'=2] {'tok'}, use_global_device_ids=true, to_apply=%region_2.2 | all-reduce | flops 16384 | bytes 98304 | tf_op jit(solution)/shard_map/while/body/eval_jaxpr/psum | solution.py:22
  37.3 0.7 dynamic_slice.163
  37.9 0.7 iota_compare_fusion.4
  38.9 16.6 %all_gather.57 = bf16[64,2048]{0,1:T(8,128)(2,1)S(1)} all-gather(bf16[64,512]{0,1:T(8,128)(2,1)S(1)} %bitcast.104), channel_id=1, replica_groups=mesh['groups'=2,'feat'=4,'layer'=2,'tok'=2] {'feat'}, dimensions={1}, use_global_device_ids=true | all-gather | bytes 327680 | tf_op jit(solution)/shard_map/while/body/eval_jaxpr/all_gather | solution.py:117
  55.6 0.5 convolution_add_fusion.2
  56.2 14.5 %all-gather.10 = bf16[4,448,64]{1,2,0:T(8,128)(2,1)S(1)} all-gather(bf16[1,448,64]{1,2,0:T(8,128)(2,1)S(1)} %fusion.61), channel_id=1, replica_groups=mesh['groups'=2,'feat'=4,'layer'=2,'tok'=2] {'feat'}, dimensions={0}, use_global_device_ids=true | all-gather | bytes 286720 | tf_op jit(solution)/shard_map/while/body/eval_jaxpr/all_gather | solution.py:18
  70.9 0.3 reshape.114
  71.2 1.2 fusion.62
  72.4 3.4 %psum.35 = f32[64,128]{1,0:T(8,128)S(1)} all-reduce(f32[64,128]{1,0:T(8,128)S(1)} %fusion.62), channel_id=1, replica_groups=mesh['groups'=2,'feat'=4,'layer'=2,'tok'=2] {'tok'}, use_global_device_ids=true, to_apply=%region_3.3 | all-reduce | flops 8192 | bytes 65536 | tf_op jit(solution)/shard_map/while/body/eval_jaxpr/psum | solution.py:22
  76.0 13.1 %all-gather.11 = bf16[256,128]{1,0:T(8,128)(2,1)S(1)} all-gather(bf16[64,128]{1,0:T(8,128)(2,1)S(1)} %get-tuple-element.762), channel_id=2, replica_groups=mesh['groups'=2,'feat'=4,'layer'=2,'tok'=2] {'feat'}, dimensions={0}, use_global_device_ids=true | all-gather | bytes 81920 | tf_op jit(solution)/shard_map/while/body/eval_jaxpr/all_gather | solution.py:7
  89.2 1.6 fusion.63
  90.8 4.1 %collective-permute-start.1 = (f32[2,64,448]{2,1,0:T(8,128)S(1)}, f32[2,64,448]{2,1,0:T(8,128)}, u32[]{:S(2)}, u32[]{:S(2)}) collective-permute-start(f32[2,64,448]{2,1,0:T(8,128)S(1)} %fusion.63), channel_id=1, source_target_pairs={{0,2},{1,3},{4,6},{5,7},{8,10},{9,11},{12,14},{13,15},{16,18},{17,... | collective-permute-start | bytes 688136 | tf_op jit(solution)/shard_map/while/body/eval_jaxpr/ppermute | solution.py:14
  94.9 1.6 select_dynamic-update-slice_fusion.5
  96.5 1.3 collective-permute-start
  97.8 3.0 %collective-permute-done = f32[64,448]{1,0:T(8,128)S(1)} collective-permute-done((f32[64,448]{1,0:T(8,128)S(1)}, f32[64,448]{1,0:T(8,128)S(1)}, u32[]{:S(2)}, u32[]{:S(2)}) %collective-permute-start) | collective-permute-done | bytes 114720 | tf_op jit(solution)/shard_map/while/body/eval_jaxpr/ppermute | solution.py:14
  101.0 14.4 %all-gather.9 = bf16[4,448,64]{1,2,0:T(8,128)(2,1)S(1)} all-gather(bf16[1,448,64]{1,2,0:T(8,128)(2,1)S(1)} %fusion.57), channel_id=1, replica_groups=mesh['groups'=2,'feat'=4,'layer'=2,'tok'=2] {'feat'}, dimensions={0}, use_global_device_ids=true | all-gather | bytes 286720 | tf_op jit(solution)/shard_map/while/body/eval_jaxpr/all_gather | solution.py:18
  115.7 0.3 reshape.113
  116.0 1.4 fusion.58
  117.4 3.6 %psum.34 = bf16[64,256]{1,0:T(8,128)(2,1)S(1)} all-reduce(f32[64,256]{1,0:T(8,128)S(1)} %fusion.58), channel_id=1, replica_groups=mesh['groups'=2,'feat'=4,'layer'=2,'tok'=2] {'tok'}, use_global_device_ids=true, to_apply=%region_2.2 | all-reduce | flops 16384 | bytes 98304 | tf_op jit(solution)/shard_map/while/body/eval_jaxpr/psum | solution.py:22
  121.0 0.7 dynamic_slice.163
  121.7 0.7 iota_compare_fusion.4
  122.7 15.6 %all_gather.57 = bf16[64,2048]{0,1:T(8,128)(2,1)S(1)} all-gather(bf16[64,512]{0,1:T(8,128)(2,1)S(1)} %bitcast.104), channel_id=1, replica_groups=mesh['groups'=2,'feat'=4,'layer'=2,'tok'=2] {'feat'}, dimensions={1}, use_global_device_ids=true | all-gather | bytes 327680 | tf_op jit(solution)/shard_map/while/body/eval_jaxpr/all_gather | solution.py:117
  138.4 0.5 convolution_add_fusion.2
  138.9 14.5 %all-gather.10 = bf16[4,448,64]{1,2,0:T(8,128)(2,1)S(1)} all-gather(bf16[1,448,64]{1,2,0:T(8,128)(2,1)S(1)} %fusion.61), channel_id=1, replica_groups=mesh['groups'=2,'feat'=4,'layer'=2,'tok'=2] {'feat'}, dimensions={0}, use_global_device_ids=true | all-gather | bytes 286720 | tf_op jit(solution)/shard_map/while/body/eval_jaxpr/all_gather | solution.py:18
  153.6 0.3 reshape.114
  153.9 1.2 fusion.62
  155.1 3.4 %psum.35 = f32[64,128]{1,0:T(8,128)S(1)} all-reduce(f32[64,128]{1,0:T(8,128)S(1)} %fusion.62), channel_id=1, replica_groups=mesh['groups'=2,'feat'=4,'layer'=2,'tok'=2] {'tok'}, use_global_device_ids=true, to_apply=%region_3.3 | all-reduce | flops 8192 | bytes 65536 | tf_op jit(solution)/shard_map/while/body/eval_jaxpr/psum | solution.py:22
  158.6 13.1 %all-gather.11 = bf16[256,128]{1,0:T(8,128)(2,1)S(1)} all-gather(bf16[64,128]{1,0:T(8,128)(2,1)S(1)} %get-tuple-element.762), channel_id=2, replica_groups=mesh['groups'=2,'feat'=4,'layer'=2,'tok'=2] {'feat'}, dimensions={0}, use_global_device_ids=true | all-gather | bytes 81920 | tf_op jit(solution)/shard_map/while/body/eval_jaxpr/all_gather | solution.py:7
  171.9 1.6 fusion.63
  173.5 5.1 %collective-permute-start.1 = (f32[2,64,448]{2,1,0:T(8,128)S(1)}, f32[2,64,448]{2,1,0:T(8,128)}, u32[]{:S(2)}, u32[]{:S(2)}) collective-permute-start(f32[2,64,448]{2,1,0:T(8,128)S(1)} %fusion.63), channel_id=1, source_target_pairs={{0,2},{1,3},{4,6},{5,7},{8,10},{9,11},{12,14},{13,15},{16,18},{17,... | collective-permute-start | bytes 688136 | tf_op jit(solution)/shard_map/while/body/eval_jaxpr/ppermute | solution.py:14
  178.6 1.7 select_dynamic-update-slice_fusion.5
  180.2 1.3 collective-permute-start
  181.5 3.0 %collective-permute-done = f32[64,448]{1,0:T(8,128)S(1)} collective-permute-done((f32[64,448]{1,0:T(8,128)S(1)}, f32[64,448]{1,0:T(8,128)S(1)}, u32[]{:S(2)}, u32[]{:S(2)}) %collective-permute-start) | collective-permute-done | bytes 114720 | tf_op jit(solution)/shard_map/while/body/eval_jaxpr/ppermute | solution.py:14
  184.7 14.4 %all-gather.9 = bf16[4,448,64]{1,2,0:T(8,128)(2,1)S(1)} all-gather(bf16[1,448,64]{1,2,0:T(8,128)(2,1)S(1)} %fusion.57), channel_id=1, replica_groups=mesh['groups'=2,'feat'=4,'layer'=2,'tok'=2] {'feat'}, dimensions={0}, use_global_device_ids=true | all-gather | bytes 286720 | tf_op jit(solution)/shard_map/while/body/eval_jaxpr/all_gather | solution.py:18
  199.4 0.3 reshape.113
  199.6 1.5 fusion.58
  201.1 3.6 %psum.34 = bf16[64,256]{1,0:T(8,128)(2,1)S(1)} all-reduce(f32[64,256]{1,0:T(8,128)S(1)} %fusion.58), channel_id=1, replica_groups=mesh['groups'=2,'feat'=4,'layer'=2,'tok'=2] {'tok'}, use_global_device_ids=true, to_apply=%region_2.2 | all-reduce | flops 16384 | bytes 98304 | tf_op jit(solution)/shard_map/while/body/eval_jaxpr/psum | solution.py:22
  204.7 0.7 dynamic_slice.163
  205.4 0.7 iota_compare_fusion.4
  206.4 15.6 %all_gather.57 = bf16[64,2048]{0,1:T(8,128)(2,1)S(1)} all-gather(bf16[64,512]{0,1:T(8,128)(2,1)S(1)} %bitcast.104), channel_id=1, replica_groups=mesh['groups'=2,'feat'=4,'layer'=2,'tok'=2] {'feat'}, dimensions={1}, use_global_device_ids=true | all-gather | bytes 327680 | tf_op jit(solution)/shard_map/while/body/eval_jaxpr/all_gather | solution.py:117
  222.0 0.5 convolution_add_fusion.2
  222.6 14.5 %all-gather.10 = bf16[4,448,64]{1,2,0:T(8,128)(2,1)S(1)} all-gather(bf16[1,448,64]{1,2,0:T(8,128)(2,1)S(1)} %fusion.61), channel_id=1, replica_groups=mesh['groups'=2,'feat'=4,'layer'=2,'tok'=2] {'feat'}, dimensions={0}, use_global_device_ids=true | all-gather | bytes 286720 | tf_op jit(solution)/shard_map/while/body/eval_jaxpr/all_gather | solution.py:18
  237.3 0.3 reshape.114
  237.6 1.2 fusion.62
  238.8 3.4 %psum.35 = f32[64,128]{1,0:T(8,128)S(1)} all-reduce(f32[64,128]{1,0:T(8,128)S(1)} %fusion.62), channel_id=1, replica_groups=mesh['groups'=2,'feat'=4,'layer'=2,'tok'=2] {'tok'}, use_global_device_ids=true, to_apply=%region_3.3 | all-reduce | flops 8192 | bytes 65536 | tf_op jit(solution)/shard_map/while/body/eval_jaxpr/psum | solution.py:22
  242.3 13.1 %all-gather.11 = bf16[256,128]{1,0:T(8,128)(2,1)S(1)} all-gather(bf16[64,128]{1,0:T(8,128)(2,1)S(1)} %get-tuple-element.762), channel_id=2, replica_groups=mesh['groups'=2,'feat'=4,'layer'=2,'tok'=2] {'feat'}, dimensions={0}, use_global_device_ids=true | all-gather | bytes 81920 | tf_op jit(solution)/shard_map/while/body/eval_jaxpr/all_gather | solution.py:7
  255.6 1.6 fusion.63
  257.1 5.1 %collective-permute-start.1 = (f32[2,64,448]{2,1,0:T(8,128)S(1)}, f32[2,64,448]{2,1,0:T(8,128)}, u32[]{:S(2)}, u32[]{:S(2)}) collective-permute-start(f32[2,64,448]{2,1,0:T(8,128)S(1)} %fusion.63), channel_id=1, source_target_pairs={{0,2},{1,3},{4,6},{5,7},{8,10},{9,11},{12,14},{13,15},{16,18},{17,... | collective-permute-start | bytes 688136 | tf_op jit(solution)/shard_map/while/body/eval_jaxpr/ppermute | solution.py:14
  262.3 1.7 select_dynamic-update-slice_fusion.5
  263.9 1.3 collective-permute-start
  265.2 3.0 %collective-permute-done = f32[64,448]{1,0:T(8,128)S(1)} collective-permute-done((f32[64,448]{1,0:T(8,128)S(1)}, f32[64,448]{1,0:T(8,128)S(1)}, u32[]{:S(2)}, u32[]{:S(2)}) %collective-permute-start) | collective-permute-done | bytes 114720 | tf_op jit(solution)/shard_map/while/body/eval_jaxpr/ppermute | solution.py:14
  268.3 1.8 copy.49
  (61 shorter events, 3.8 us)
Async XLA Ops:
  0.6 1.0 copy-start
  9.8 3.5 %copy-start.2 = (f32[128,1,448]{0,2,1:T(8,128)S(1)}, f32[128,1,448]{0,2,1:T(8,128)}, u32[]{:S(2)}) copy-start(f32[128,1,448]{0,2,1:T(8,128)} %param.17) | copy-start | bytes 688132
  9.8 3.7 %copy-start.3 = (f32[1,128,1,448]{1,3,2,0:T(8,128)S(1)}, f32[1,128,1,448]{1,3,2,0:T(8,128)}, u32[]{:S(2)}) copy-start(f32[1,128,1,448]{1,3,2,0:T(8,128)} %param.27) | copy-start | bytes 688132
  9.8 6.0 %copy-start.4 = (f32[1,128]{1,0:T(1,128)S(1)}, f32[1,128]{1,0:T(1,128)}, u32[]{:S(2)}) copy-start(f32[1,128]{1,0:T(1,128)} %param.25) | copy-start | bytes 1540
  9.8 6.0 %copy-start.5 = (f32[1,128]{1,0:T(1,128)S(1)}, f32[1,128]{1,0:T(1,128)}, u32[]{:S(2)}) copy-start(f32[1,128]{1,0:T(1,128)} %param.18) | copy-start | bytes 1540
  9.9 6.0 %copy-start.6 = (s32[2]{0:T(128)S(1)}, s32[2]{0:T(128)}, u32[]{:S(2)}) copy-start(s32[2]{0:T(128)} %param.21) | copy-start | bytes 28
  9.9 6.0 %copy-start.7 = (f32[1,128]{1,0:T(1,128)S(1)}, f32[1,128]{1,0:T(1,128)}, u32[]{:S(2)}) copy-start(f32[1,128]{1,0:T(1,128)} %param.19) | copy-start | bytes 1540
  90.8 10.1 %collective-permute-start.1 = (f32[2,64,448]{2,1,0:T(8,128)S(1)}, f32[2,64,448]{2,1,0:T(8,128)}, u32[]{:S(2)}, u32[]{:S(2)}) collective-permute-start(f32[2,64,448]{2,1,0:T(8,128)S(1)} %fusion.63), channel_id=1, source_target_pairs={{0,2},{1,3},{4,6},{5,7},{8,10},{9,11},{12,14},{13,15},{16,18},{17,... | collective-permute-start | bytes 688136 | tf_op jit(solution)/shard_map/while/body/eval_jaxpr/ppermute | solution.py:14
  96.5 4.3 %collective-permute-start = (f32[64,448]{1,0:T(8,128)S(1)}, f32[64,448]{1,0:T(8,128)S(1)}, u32[]{:S(2)}, u32[]{:S(2)}) collective-permute-start(f32[64,448]{1,0:T(8,128)S(1)} %get-tuple-element.763), channel_id=1, source_target_pairs={{0,2},{1,3},{4,6},{5,7},{8,10},{9,11},{12,14},{13,15},{16,18},{17,... | collective-permute-start | bytes 344072 | tf_op jit(solution)/shard_map/while/body/eval_jaxpr/ppermute | solution.py:14
  173.5 11.1 %collective-permute-start.1 = (f32[2,64,448]{2,1,0:T(8,128)S(1)}, f32[2,64,448]{2,1,0:T(8,128)}, u32[]{:S(2)}, u32[]{:S(2)}) collective-permute-start(f32[2,64,448]{2,1,0:T(8,128)S(1)} %fusion.63), channel_id=1, source_target_pairs={{0,2},{1,3},{4,6},{5,7},{8,10},{9,11},{12,14},{13,15},{16,18},{17,... | collective-permute-start | bytes 688136 | tf_op jit(solution)/shard_map/while/body/eval_jaxpr/ppermute | solution.py:14
  180.2 4.3 %collective-permute-start = (f32[64,448]{1,0:T(8,128)S(1)}, f32[64,448]{1,0:T(8,128)S(1)}, u32[]{:S(2)}, u32[]{:S(2)}) collective-permute-start(f32[64,448]{1,0:T(8,128)S(1)} %get-tuple-element.763), channel_id=1, source_target_pairs={{0,2},{1,3},{4,6},{5,7},{8,10},{9,11},{12,14},{13,15},{16,18},{17,... | collective-permute-start | bytes 344072 | tf_op jit(solution)/shard_map/while/body/eval_jaxpr/ppermute | solution.py:14
  257.1 11.1 %collective-permute-start.1 = (f32[2,64,448]{2,1,0:T(8,128)S(1)}, f32[2,64,448]{2,1,0:T(8,128)}, u32[]{:S(2)}, u32[]{:S(2)}) collective-permute-start(f32[2,64,448]{2,1,0:T(8,128)S(1)} %fusion.63), channel_id=1, source_target_pairs={{0,2},{1,3},{4,6},{5,7},{8,10},{9,11},{12,14},{13,15},{16,18},{17,... | collective-permute-start | bytes 688136 | tf_op jit(solution)/shard_map/while/body/eval_jaxpr/ppermute | solution.py:14
  263.9 4.3 %collective-permute-start = (f32[64,448]{1,0:T(8,128)S(1)}, f32[64,448]{1,0:T(8,128)S(1)}, u32[]{:S(2)}, u32[]{:S(2)}) collective-permute-start(f32[64,448]{1,0:T(8,128)S(1)} %get-tuple-element.763), channel_id=1, source_target_pairs={{0,2},{1,3},{4,6},{5,7},{8,10},{9,11},{12,14},{13,15},{16,18},{17,... | collective-permute-start | bytes 344072 | tf_op jit(solution)/shard_map/while/body/eval_jaxpr/ppermute | solution.py:14
  268.3 1.8 copy-start.1
